TPU v7x, 128 devices: a whole 4x4x4 slice. The times are simulated.
128 devices in a mesh: sky: 16 (over z, y), exp: 8 (over x, core).
Axes of the slice: x: 4, y: 4, z: 4, core: 2. Of those that a mesh axis runs over, the one named last changes fastest.
Arguments:
- sky_model: bfloat16 [4096, 1024], P('sky'), may hold values from -6 to 6
- exposure_data: bfloat16 [2048, 128, 128], P(('sky', 'exp')), may hold values from -6 to 6
- pixel_mask: int32 [2048, 128, 128], P(('sky', 'exp')), may hold values 0 or 1
- block_owner: int32 [2048, 1], P(('sky', 'exp')), may hold values from 0 to 15; in each aligned block of 16 rows (0 to 15, 16 to 31, ...) at most 2 rows name the same one
- block_local: int32 [2048], P(('sky', 'exp')), may hold values from 0 to 15
- psf_cell: int32 [2048], P(('sky', 'exp')), may hold values from 0 to 15
- psf_table: bfloat16 [128, 1681], P('exp'), may hold values from -0.15625 to 0.15625
Outputs:
- model_grad: float32 [4096, 1024], P('sky', 'exp')
- residual: bfloat16 [2048, 128, 128], P(('sky', 'exp'))
Inputs may be any that keep to these rules, and one draw needn't show every extreme that they name: `block_owner`: among the pieces of one device no sky index is named more than 2 times.
All inputs are finite; a program needn't handle non-finite values. No bound on the sum of `pixel_mask` on one device may be relied on, other than what follows from the above.
Results may differ from a plain program's by a relative error of at most 0.014.
Values may be sent and summed in bfloat16 or wider, within the bound.
No kernel may reach another device: no remote copies, remote signals or barrier semaphores. Data moves between devices by JAX's collectives and lax.ppermute only.
A program may use at most 64 MiB of HBM per device.

v0:
```python
import jax
import jax.numpy as jnp
from jax import lax
from jax.sharding import PartitionSpec as P

B = 128
PSF = 41
HALO = 20
CAP = 2


def from_behind(x, axis, by):
    devices = lax.axis_size(axis)
    pairs = [(i, i + by) for i in range(devices) if 0 <= i + by < devices]
    return lax.ppermute(x, axis, pairs)


def banded_table(out_cols):
    width = out_cols + PSF - 1
    tap_index = lax.broadcasted_iota(jnp.int32, (PSF, width, out_cols), 0)
    column = lax.broadcasted_iota(jnp.int32, (PSF, width, out_cols), 1)
    target = lax.broadcasted_iota(jnp.int32, (PSF, width, out_cols), 2)
    return (column - target == tap_index).astype(jnp.bfloat16)


def correlate(field, kernel, table, out_rows):
    out_cols = table.shape[2]
    width = field.shape[1]
    banded = jnp.einsum("ab,bcj->caj", kernel, table, preferred_element_type=jnp.float32).astype(
        jnp.bfloat16
    )
    spread = jnp.dot(
        field, banded.reshape(width, PSF * out_cols), preferred_element_type=jnp.float32
    )
    total = spread[0:out_rows, 0:out_cols]
    for offset in range(1, PSF):
        total = (
            total + spread[offset : offset + out_rows, offset * out_cols : (offset + 1) * out_cols]
        )
    return total


def fold_blocks(per_block, block_rows, per_row):
    extent = B + 2 * HALO
    margin = 2 * HALO
    grid = per_block.reshape(block_rows, per_row, extent, extent)
    col_main = grid[..., :B].transpose(0, 2, 1, 3).reshape(block_rows, extent, per_row * B)
    col_tail = jnp.pad(grid[..., B:], ((0, 0), (0, 0), (0, 0), (0, B - margin)))
    col_tail = col_tail.transpose(0, 2, 1, 3).reshape(block_rows, extent, per_row * B)
    width = per_row * B + margin
    columns = (
        jnp.pad(col_main, ((0, 0), (0, 0), (0, margin)))
        + jnp.pad(col_tail, ((0, 0), (0, 0), (B, 0)))[:, :, :width]
    )
    row_main = columns[:, :B].reshape(block_rows * B, width)
    row_tail = jnp.pad(columns[:, B:], ((0, 0), (0, B - margin), (0, 0))).reshape(
        block_rows * B, width
    )
    height = block_rows * B + margin
    return jnp.pad(row_main, ((0, margin), (0, 0))) + jnp.pad(row_tail, ((B, 0), (0, 0)))[:height]


def shards(sky_model, exposure_data, pixel_mask, block_owner, block_local, psf_cell, psf_table):
    sky_count = lax.axis_size("sky")
    extent = B + 2 * HALO
    stripe_rows = sky_model.shape[0]
    stripe_cols = sky_model.shape[1]
    per_row = stripe_cols // B
    block_rows = stripe_rows // B
    block_total = block_rows * per_row
    piece_count = exposure_data.shape[0]
    slot_total = sky_count * CAP
    owner_sky = block_owner[:, 0]
    earlier = lax.broadcasted_iota(jnp.int32, (piece_count, piece_count), 1) < lax.broadcasted_iota(
        jnp.int32, (piece_count, piece_count), 0
    )
    same_owner = owner_sky[:, None] == owner_sky[None, :]
    rank_within = jnp.sum((same_owner & earlier).astype(jnp.int32), axis=1)
    slot_index = owner_sky * CAP + rank_within
    requests = (
        jnp.full((slot_total,), -1, jnp.int32)
        .at[slot_index]
        .set(block_local)
        .reshape(sky_count, CAP)
    )
    cell_count = psf_table.shape[0]
    cell_onehot = (psf_cell[:, None] == lax.broadcasted_iota(jnp.int32, (1, cell_count), 1)).astype(
        jnp.bfloat16
    )
    kernels_flat = jnp.dot(cell_onehot, psf_table, preferred_element_type=jnp.float32).astype(
        jnp.bfloat16
    )
    forward_table = banded_table(B)
    adjoint_table = banded_table(extent)

    def per_piece(item):
        patch, kernel, observed, keep = item
        predicted = correlate(patch, kernel, forward_table, B)
        residual = (keep.astype(jnp.float32) * (predicted - observed.astype(jnp.float32))).astype(
            jnp.bfloat16
        )
        widened = jnp.pad(residual, 2 * HALO)
        adjoint = correlate(widened, kernel[::-1, ::-1], adjoint_table, extent)
        return (residual, adjoint)

    whole = lax.all_gather(sky_model, "sky", axis=0, tiled=True)
    padded = jnp.pad(whole, HALO)
    row_start = (owner_sky * block_rows + block_local // per_row) * B
    col_start = block_local % per_row * B

    def cut_patch(row_first, col_first):
        return lax.dynamic_slice(padded, (row_first, col_first), (extent, extent))

    patches = jax.vmap(cut_patch)(row_start, col_start)
    kernels = kernels_flat.reshape(piece_count, PSF, PSF)
    residuals, adjoints = lax.map(per_piece, (patches, kernels, exposure_data, pixel_mask))
    outgoing = jnp.zeros((slot_total, extent, extent), jnp.float32).at[slot_index].set(adjoints)
    outgoing = outgoing.reshape(sky_count, CAP, extent, extent)
    received, received_ids = (
        lax.all_to_all(
            outgoing.astype(jnp.bfloat16), "sky", split_axis=0, concat_axis=0, tiled=True
        ).astype(outgoing.dtype),
        lax.all_to_all(requests, "sky", split_axis=0, concat_axis=0, tiled=True),
    )
    contributions = received.reshape(slot_total, extent, extent)
    asked_ids = received_ids.reshape(slot_total)
    selector = (asked_ids[:, None] == lax.broadcasted_iota(jnp.int32, (1, block_total), 1)).astype(
        jnp.float32
    )
    per_block = jnp.einsum("nl,nuv->luv", selector, contributions, precision=lax.Precision.HIGHEST)
    canvas = fold_blocks(per_block, block_rows, per_row)
    core = canvas[:, HALO : HALO + stripe_cols]
    from_below = from_behind(core[:HALO].astype(jnp.bfloat16), "sky", -1).astype(jnp.float32)
    from_above = from_behind(core[stripe_rows + HALO :].astype(jnp.bfloat16), "sky", 1).astype(
        jnp.float32
    )
    middle = core[HALO : stripe_rows + HALO]
    folded = (
        middle
        + jnp.pad(from_above, ((0, stripe_rows - HALO), (0, 0)))
        + jnp.pad(from_below, ((stripe_rows - HALO, 0), (0, 0)))
    )
    gradient = lax.psum_scatter(
        folded.astype(jnp.bfloat16), "exp", scatter_dimension=1, tiled=True
    ).astype(jnp.float32)
    return (gradient, residuals)


def solution(mesh):
    in_specs = (
        P("sky", None),
        P(("sky", "exp"), None, None),
        P(("sky", "exp"), None, None),
        P(("sky", "exp"), None),
        P(("sky", "exp")),
        P(("sky", "exp")),
        P("exp", None),
    )
    out_specs = (P("sky", "exp"), P(("sky", "exp"), None, None))
    return jax.shard_map(shards, mesh=mesh, in_specs=in_specs, out_specs=out_specs, check_vma=False)
```

profile of v0, /device:TPU:0, one launch (start us, length us, event | category | flops | bytes accessed | tf_op | source)
XLA Modules:
  0.0 443.7 jit_solution(5079500784704721920)
XLA Ops:
  10.9 8.1 %all-to-all-start = ((s32[16,1,2]{2,1,0:T(1,128)}), s32[16,1,2]{2,1,0:T(1,128)S(1)}, u32[]{:S(2)}, u32[]{:S(2)}) async-start(s32[16,1,2]{2,1,0:T(1,128)} %bitcast.3), calls=%async_computation | async-start | bytes 16384 | tf_op jit(solution)/shard_map/all_to_all | solution.py:123
  20.9 62.6 %all-gather.2.cloned.1.call-done = bf16[4096,1024]{1,0:T(8,128)(2,1)} async-done(((bf16[256,1024]{1,0:T(8,128)(2,1)}), bf16[4096,1024]{1,0:T(8,128)(2,1)}) %all-gather.2.cloned.1.call-update) | async-done | bytes 8388624 | tf_op jit(solution)/shard_map/all_gather | solution.py:106
  83.5 14.8 %pad.49 = bf16[4136,1064]{1,0:T(8,128)(2,1)} pad(bf16[4096,1024]{1,0:T(8,128)(2,1)} %all-gather.2.cloned.1.call-done, bf16[]{:T(256)} %constant.73.clone.1), padding=20_20x20_20 | pad | bytes 17190018 | tf_op jit(solution)/shard_map/jit(_pad)/pad | solution.py:107
  98.3 58.3 %while.16 = (s32[]{:T(128)}, bf16[4136,1064]{1,0:T(8,128)(2,1)}, s32[16,2]{0,1:T(2,128)S(1)}, bf16[16,168,168]{2,1,0:T(8,128)(2,1)}, s32[]{:T(128)}) while((s32[]{:T(128)}, bf16[4136,1064]{1,0:T(8,128)(2,1)}, s32[16,2]{0,1:T(2,128)S(1)}, bf16[16,168,168]{2,1,0:T(8,128)(2,1)}, s32[]{:T(128)}) %tuple.53), condition=%wide.while_cond, body=%wide.while_body.sunk | while | flops 2 | bytes 173665 | solution.py:112
  99.0 3.0 bitcast_dynamic-update-slice_fusion.4
  102.6 3.0 bitcast_dynamic-update-slice_fusion.4
  106.3 3.0 bitcast_dynamic-update-slice_fusion.4
  109.9 3.0 bitcast_dynamic-update-slice_fusion.4
  113.5 3.0 bitcast_dynamic-update-slice_fusion.4
  117.2 3.0 bitcast_dynamic-update-slice_fusion.4
  120.8 3.0 bitcast_dynamic-update-slice_fusion.4
  124.5 3.0 bitcast_dynamic-update-slice_fusion.4
  128.1 3.0 bitcast_dynamic-update-slice_fusion.4
  131.8 3.0 bitcast_dynamic-update-slice_fusion.4
  135.4 3.0 bitcast_dynamic-update-slice_fusion.4
  139.1 3.0 bitcast_dynamic-update-slice_fusion.4
  142.7 3.0 bitcast_dynamic-update-slice_fusion.4
  146.4 3.0 bitcast_dynamic-update-slice_fusion.4
  150.0 3.0 bitcast_dynamic-update-slice_fusion.4
  153.7 3.0 bitcast_dynamic-update-slice_fusion.4
  156.6 157.8 %while.17 = (s32[]{:T(128)}, bf16[16,128,128]{2,1,0:T(8,128)(2,1)}, f32[16,168,168]{2,1,0:T(8,128)S(1)}, s32[16,128,128]{2,1,0:T(8,128)}, bf16[16,168,168]{2,1,0...) while((s32[]{:T(128)}, bf16[16,128,128]{2,1,0:T(8,128)(2,1)}, ...), condition=%wide.region_3.4_spmd.clone, body=%wide.region_2.3_spmd.clone.sunk | while | flops 1093145856 | bytes 34470920 | solution.py:116
  174.4 1.9 fusion.82
  314.4 2.8 broadcast_in_dim.36
  317.2 4.1 scatter_fusion
  321.4 2.8 convert_element_type.99
  324.2 3.7 copy.17
  327.9 5.2 %all-to-all-start.1 = ((bf16[16,2,168,168]{3,1,2,0:T(2,128)(2,1)}), bf16[16,2,168,168]{3,1,2,0:T(2,128)(2,1)S(1)}, u32[]{:S(2)}, u32[]{:S(2)}) async-start(bf16[16,2,168,168]{3,1,2,0:T(2,128)(2,1)} %copy.17), calls=%async_computation.1 | async-start | bytes 5505024 | tf_op jit(solution)/shard_map/all_to_all | solution.py:120
  334.7 40.4 %all-to-all-done.1 = bf16[16,2,168,168]{3,1,2,0:T(2,128)(2,1)S(1)} async-done(((bf16[16,2,168,168]{3,1,2,0:T(2,128)(2,1)}), bf16[16,2,168,168]{3,1,2,0:T(2,128)(2,1)S(1)}, u32[]{:S(2)}, u32[]{:S(2)}) %all-to-all-start.1) | async-done | bytes 1806368 | tf_op jit(solution)/shard_map/all_to_all | solution.py:120
  375.1 4.7 %copy.18 = bf16[16,2,168,168]{3,1,0,2:T(2,128)(2,1)} copy(bf16[16,2,168,168]{3,1,2,0:T(2,128)(2,1)S(1)} %all-to-all-done.1) | data formatting | bytes 3612672 | tf_op jit(solution)/shard_map/all_to_all | solution.py:120
  379.8 5.7 %reshape.115 = bf16[32,168,168,1]{2,0,1,3:T(8,128)(2,1)S(1)} reshape(bf16[16,2,168,168]{3,1,0,2:T(2,128)(2,1)} %copy.18) | data formatting | bytes 3612672 | tf_op jit(solution)/shard_map/reshape | solution.py:125
  395.3 4.3 collective-permute-done.1
  400.9 34.3 %reduce-scatter.4.cloned.1.call-done = bf16[128,256]{1,0:T(8,128)(2,1)} async-done(((bf16[1024,256]{1,0:T(8,128)(2,1)}), bf16[128,256]{1,0:T(8,128)(2,1)}) %reduce-scatter.4.cloned.1.call-update) | async-done | bytes 65552
  (218 shorter events, 185.5 us)
Async XLA Ops:
  7.2 11.9 %copy-start = (bf16[16,1681]{1,0:T(8,128)(2,1)S(1)}, bf16[16,1681]{1,0:T(8,128)(2,1)}, u32[]{:S(2)}) copy-start(bf16[16,1681]{1,0:T(8,128)(2,1)} %param.15) | copy-start | bytes 161380
  7.2 76.3 %all-gather.2.cloned.1.call-start = ((), (), s32[]{:S(2)}) async-start(), calls=%async_computation.3 | async-start | bytes 8912896 | tf_op jit(solution)/shard_map/all_gather | solution.py:106
  10.9 316.9 %all-to-all-start = ((s32[16,1,2]{2,1,0:T(1,128)}), s32[16,1,2]{2,1,0:T(1,128)S(1)}, u32[]{:S(2)}, u32[]{:S(2)}) async-start(s32[16,1,2]{2,1,0:T(1,128)} %bitcast.3), calls=%async_computation | async-start | bytes 16384 | tf_op jit(solution)/shard_map/all_to_all | solution.py:123
  327.9 47.2 %all-to-all-start.1 = ((bf16[16,2,168,168]{3,1,2,0:T(2,128)(2,1)}), bf16[16,2,168,168]{3,1,2,0:T(2,128)(2,1)S(1)}, u32[]{:S(2)}, u32[]{:S(2)}) async-start(bf16[16,2,168,168]{3,1,2,0:T(2,128)(2,1)} %copy.17), calls=%async_computation.1 | async-start | bytes 5505024 | tf_op jit(solution)/shard_map/all_to_all | solution.py:120
  333.1 102.1 %reduce-scatter.4.cloned.1.call-start = ((), (), s32[]{:S(2)}) async-start(), calls=%async_computation.4 | async-start | bytes 589824
  392.0 44.8 %copy-start.1 = (bf16[16,1681]{1,0:T(8,128)(2,1)S(1)}, bf16[16,1681]{1,0:T(8,128)(2,1)}, u32[]{:S(2)}) copy-start(bf16[16,1681]{1,0:T(8,128)(2,1)} %param.15) | copy-start | bytes 161380
  392.3 3.0 collective-permute-start
  393.6 6.0 %collective-permute-start.1 = (bf16[20,1024]{1,0:T(8,128)(2,1)S(1)}, bf16[20,1024]{1,0:T(8,128)(2,1)S(1)}, u32[]{:S(2)}, u32[]{:S(2)}) collective-permute-start(bf16[20,1024]{1,0:T(8,128)(2,1)S(1)} %get-tuple-element.172), channel_id=1, source_target_pairs={{8,0},{16,8},{24,16},{32,24},{40,32},{48,40},{56,48},{64,56},{72,6... | collective-permute-start | bytes 122888 | tf_op jit(solution)/shard_map/ppermute | solution.py:15
Sparse Core Ops, SparseCore 0:
  10.2 73.3 all-gather.1
  401.0 34.1 reduce-scatter.3
where the time goes:
time: 446 us; the launch traced here: 444 us
  waiting for transfers between devices  143 us (32%)
  local copies, waits for them, and re-layouts  125 us (28%)
  matrix products  77.6 us (17%)
  other arithmetic  67.5 us (15%)
  starting transfers between devices  16.3 us (4%)
  between operations  14.3 us (3%)
    all_gather x1, waiting for transfers between devices, shards(): whole = lax.all_gather(sky_model, 'sky', axis=0, tiled=True)  62.6 us
    dynamic_update_slice x32, other arithmetic, shards(): lax.map(per_piece, (patches, kernels, exposure_data, pixel_mask))  59 us
    gather x48, local copies, waits for them, and re-layouts  58.3 us
    dot_general x32, matrix products, correlate(): jnp.dot(field, banded.reshape(width, PSF * out_cols), preferred_element_t...  45.9 us
    all_to_all x1, waiting for transfers between devices, shards(): lax.all_to_all(outgoing.astype(jnp.bfloat16), 'sky', split_axis=0, concat...  40.4 us
    unnamed x3, waiting for transfers between devices  35 us
    dot_general x32, matrix products, correlate(): jnp.einsum('ab,bcj->caj', kernel, table, preferred_element_type=jnp.float32)  30.2 us
    convert_element_type x16, local copies, waits for them, and re-layouts, correlate(): jnp.einsum('ab,bcj->caj', kernel, table, preferred_element_type=jnp.float32)  20.1 us
  transfers between devices with their start and end apart: 6, of which 5 were waited for; matrix products, arithmetic and copies ran while one was open for 56% of the time, Pallas kernels for 0%

commit v1 on v0

--- a/solution.py
+++ b/solution.py
@@ -2,6 +2,7 @@
 import jax.numpy as jnp
 from jax import lax
 from jax.sharding import PartitionSpec as P
+from jax.lax import all_to_all, axis_size
 
 B = 128
 PSF = 41
@@ -103,7 +104,9 @@
         adjoint = correlate(widened, kernel[::-1, ::-1], adjoint_table, extent)
         return (residual, adjoint)
 
-    whole = lax.all_gather(sky_model, "sky", axis=0, tiled=True)
+    whole = jnp.concatenate(
+        all_to_all(jnp.stack([sky_model] * axis_size("sky"), 0), "sky", 0, 0), 0
+    )
     padded = jnp.pad(whole, HALO)
     row_start = (owner_sky * block_rows + block_local // per_row) * B
     col_start = block_local % per_row * B

time: 446 us -> 508 us (1.14)
  waiting for transfers between devices: 143 us -> 197 us
  starting transfers between devices: 16.3 us -> 24 us
    all_to_all x0 -> x1, waiting for transfers between devices: none -> 122 us  [shards(): all_to_all(jnp.stack([sky_model] * axis_size('sky'), 0), 'sky', 0, 0)]
    all_gather x1 -> x0, waiting for transfers between devices: 62.6 us -> none  [shards(): whole = lax.all_gather(sky_model, 'sky', axis=0, tiled=True)]
    all_to_all x0 -> x1, starting transfers between devices: none -> 8.31 us  [shards(): all_to_all(jnp.stack([sky_model] * axis_size('sky'), 0), 'sky', 0, 0)]
    another operation x0 -> x1, local copies, waits for them, and re-layouts: none -> 5.36 us  [shards(): jnp.stack([sky_model] * axis_size('sky'), 0)]
    unnamed x3 -> x2, waiting for transfers between devices: 35 us -> 34.6 us
  transfers between devices with their start and end apart: 6 -> 6, of which waited for: 5 -> 5; matrix products, arithmetic and copies ran while one was open for 56% -> 48% of each run, Pallas kernels for 0% -> 0%
where the time goes in v1:
time: 508 us; the launch traced here: 505 us
  waiting for transfers between devices  197 us (39%)
  local copies, waits for them, and re-layouts  127 us (25%)
  matrix products  76.9 us (15%)
  other arithmetic  65.4 us (13%)
  starting transfers between devices  24 us (5%)
  between operations  14.3 us (3%)
    all_to_all x1, waiting for transfers between devices, shards(): all_to_all(jnp.stack([sky_model] * axis_size('sky'), 0), 'sky', 0, 0)  122 us
    dynamic_update_slice x32, other arithmetic, shards(): lax.map(per_piece, (patches, kernels, exposure_data, pixel_mask))  59 us
    gather x48, local copies, waits for them, and re-layouts  55.3 us
    dot_general x32, matrix products, correlate(): jnp.dot(field, banded.reshape(width, PSF * out_cols), preferred_element_t...  45.9 us
    all_to_all x1, waiting for transfers between devices, shards(): lax.all_to_all(outgoing.astype(jnp.bfloat16), 'sky', split_axis=0, concat...  35.6 us
    unnamed x2, waiting for transfers between devices  34.6 us
    dot_general x32, matrix products, correlate(): jnp.einsum('ab,bcj->caj', kernel, table, preferred_element_type=jnp.float32)  30.2 us
    convert_element_type x16, local copies, waits for them, and re-layouts, correlate(): jnp.einsum('ab,bcj->caj', kernel, table, preferred_element_type=jnp.float32)  20.1 us
  transfers between devices with their start and end apart: 6, of which 5 were waited for; matrix products, arithmetic and copies ran while one was open for 48% of the time, Pallas kernels for 0%

profile of v1, /device:TPU:0, one launch (start us, length us, event | category | flops | bytes accessed | tf_op | source)
XLA Modules:
  0.0 505.1 jit_solution(705098838889908942)
XLA Ops:
  7.2 5.4 %stack.2 = bf16[16,256,1024]{2,1,0:T(8,128)(2,1)} broadcast(bf16[256,1024]{1,0:T(8,128)(2,1)} %param.9), dimensions={1,2} | broadcast | bytes 8912896 | tf_op jit(solution)/shard_map/stack | solution.py:108
  12.5 8.3 %all-to-all-start.1 = ((bf16[16,256,1024]{2,1,0:T(8,128)(2,1)}), bf16[16,256,1024]{2,1,0:T(8,128)(2,1)}, u32[]{:S(2)}, u32[]{:S(2)}) async-start(bf16[16,256,1024]{2,1,0:T(8,128)(2,1)} %stack.2), calls=%async_computation.1 | async-start | bytes 16777216 | tf_op jit(solution)/shard_map/all_to_all | solution.py:108
  22.9 122.0 %all-to-all-done.1 = bf16[16,256,1024]{2,1,0:T(8,128)(2,1)} async-done(((bf16[16,256,1024]{2,1,0:T(8,128)(2,1)}), bf16[16,256,1024]{2,1,0:T(8,128)(2,1)}, u32[]{:S(2)}, u32[]{:S(2)}) %all-to-all-start.1) | async-done | bytes 8388640 | tf_op jit(solution)/shard_map/all_to_all | solution.py:108
  144.9 5.7 %all-to-all-start = ((s32[16,1,2]{2,1,0:T(1,128)}), s32[16,1,2]{2,1,0:T(1,128)S(1)}, u32[]{:S(2)}, u32[]{:S(2)}) async-start(s32[16,1,2]{2,1,0:T(1,128)} %bitcast.3), calls=%async_computation | async-start | bytes 16384 | tf_op jit(solution)/shard_map/all_to_all | solution.py:126
  150.6 14.8 %pad.49 = bf16[4136,1064]{1,0:T(8,128)(2,1)} pad(bf16[4096,1024]{1,0:T(8,128)(2,1)} %bitcast.6, bf16[]{:T(256)} %constant.73.clone.1), padding=20_20x20_20 | pad | bytes 17190018 | tf_op jit(solution)/shard_map/jit(_pad)/pad | solution.py:110
  165.3 55.4 %while.16 = (s32[]{:T(128)}, bf16[4136,1064]{1,0:T(8,128)(2,1)}, s32[16,2]{0,1:T(2,128)S(1)}, bf16[16,168,168]{2,1,0:T(8,128)(2,1)}, s32[]{:T(128)}) while((s32[]{:T(128)}, bf16[4136,1064]{1,0:T(8,128)(2,1)}, s32[16,2]{0,1:T(2,128)S(1)}, bf16[16,168,168]{2,1,0:T(8,128)(2,1)}, s32[]{:T(128)}) %tuple.53), condition=%wide.while_cond, body=%wide.while_body.sunk | while | flops 2 | bytes 173665 | solution.py:115
  166.0 2.8 bitcast_dynamic-update-slice_fusion.4
  169.4 2.8 bitcast_dynamic-update-slice_fusion.4
  172.9 2.8 bitcast_dynamic-update-slice_fusion.4
  176.4 2.8 bitcast_dynamic-update-slice_fusion.4
  179.8 2.8 bitcast_dynamic-update-slice_fusion.4
  183.3 2.8 bitcast_dynamic-update-slice_fusion.4
  190.2 2.8 bitcast_dynamic-update-slice_fusion.4
  193.6 2.8 bitcast_dynamic-update-slice_fusion.4
  197.1 2.8 bitcast_dynamic-update-slice_fusion.4
  200.6 2.8 bitcast_dynamic-update-slice_fusion.4
  204.0 2.8 bitcast_dynamic-update-slice_fusion.4
  207.5 2.8 bitcast_dynamic-update-slice_fusion.4
  210.9 2.8 bitcast_dynamic-update-slice_fusion.4
  214.4 2.8 bitcast_dynamic-update-slice_fusion.4
  217.9 2.8 bitcast_dynamic-update-slice_fusion.4
  220.7 157.8 %while.17 = (s32[]{:T(128)}, bf16[16,128,128]{2,1,0:T(8,128)(2,1)}, f32[16,168,168]{2,1,0:T(8,128)S(1)}, s32[16,128,128]{2,1,0:T(8,128)}, bf16[16,168,168]{2,1,0...) while((s32[]{:T(128)}, bf16[16,128,128]{2,1,0:T(8,128)(2,1)}, ...), condition=%wide.region_3.4_spmd.clone, body=%wide.region_2.3_spmd.clone.sunk | while | flops 1093145856 | bytes 34470920 | solution.py:119
  378.4 2.8 broadcast_in_dim.36
  381.3 4.1 scatter_fusion
  385.4 2.8 convert_element_type.99
  388.3 3.7 copy.17
  391.9 7.2 %all-to-all-start.2 = ((bf16[16,2,168,168]{3,1,2,0:T(2,128)(2,1)}), bf16[16,2,168,168]{3,1,2,0:T(2,128)(2,1)S(1)}, u32[]{:S(2)}, u32[]{:S(2)}) async-start(bf16[16,2,168,168]{3,1,2,0:T(2,128)(2,1)} %copy.17), calls=%async_computation.2 | async-start | bytes 5505024 | tf_op jit(solution)/shard_map/all_to_all | solution.py:123
  400.7 35.6 %all-to-all-done.2 = bf16[16,2,168,168]{3,1,2,0:T(2,128)(2,1)S(1)} async-done(((bf16[16,2,168,168]{3,1,2,0:T(2,128)(2,1)}), bf16[16,2,168,168]{3,1,2,0:T(2,128)(2,1)S(1)}, u32[]{:S(2)}, u32[]{:S(2)}) %all-to-all-start.2) | async-done | bytes 1806368 | tf_op jit(solution)/shard_map/all_to_all | solution.py:123
  436.2 4.7 copy.18
  440.9 5.7 %reshape.121 = bf16[32,168,168,1]{2,0,1,3:T(8,128)(2,1)S(1)} reshape(bf16[16,2,168,168]{3,1,0,2:T(2,128)(2,1)} %copy.18) | data formatting | bytes 3612672 | tf_op jit(solution)/shard_map/reshape | solution.py:128
  456.5 4.3 collective-permute-done.1
  462.0 34.6 %reduce-scatter.4.cloned.1.call-done = bf16[128,256]{1,0:T(8,128)(2,1)} async-done(((bf16[1024,256]{1,0:T(8,128)(2,1)}), bf16[128,256]{1,0:T(8,128)(2,1)}) %reduce-scatter.4.cloned.1.call-update) | async-done | bytes 65552
  (224 shorter events, 186.3 us)
Async XLA Ops:
  7.2 13.7 %copy-start = (bf16[16,1681]{1,0:T(8,128)(2,1)S(1)}, bf16[16,1681]{1,0:T(8,128)(2,1)}, u32[]{:S(2)}) copy-start(bf16[16,1681]{1,0:T(8,128)(2,1)} %param.15) | copy-start | bytes 161380
  12.5 8.4 %copy-start.2 = (s32[16]{0:T(128)S(1)}, s32[16]{0:T(128)}, u32[]{:S(2)}) copy-start(s32[16]{0:T(128)} %param.14) | copy-start | bytes 196
  12.5 8.8 %copy-start.3 = (s32[16,1]{0,1:T(1,128)S(1)}, s32[16,1]{0,1:T(1,128)}, u32[]{:S(2)}) copy-start(s32[16,1]{0,1:T(1,128)} %param.12) | copy-start | bytes 196
  12.5 9.0 %copy-start.4 = (s32[16]{0:T(128)S(1)}, s32[16]{0:T(128)}, u32[]{:S(2)}) copy-start(s32[16]{0:T(128)} %param.13) | copy-start | bytes 196
  12.5 132.3 %all-to-all-start.1 = ((bf16[16,256,1024]{2,1,0:T(8,128)(2,1)}), bf16[16,256,1024]{2,1,0:T(8,128)(2,1)}, u32[]{:S(2)}, u32[]{:S(2)}) async-start(bf16[16,256,1024]{2,1,0:T(8,128)(2,1)} %stack.2), calls=%async_computation.1 | async-start | bytes 16777216 | tf_op jit(solution)/shard_map/all_to_all | solution.py:108
  144.9 247.0 %all-to-all-start = ((s32[16,1,2]{2,1,0:T(1,128)}), s32[16,1,2]{2,1,0:T(1,128)S(1)}, u32[]{:S(2)}, u32[]{:S(2)}) async-start(s32[16,1,2]{2,1,0:T(1,128)} %bitcast.3), calls=%async_computation | async-start | bytes 16384 | tf_op jit(solution)/shard_map/all_to_all | solution.py:126
  391.9 44.3 %all-to-all-start.2 = ((bf16[16,2,168,168]{3,1,2,0:T(2,128)(2,1)}), bf16[16,2,168,168]{3,1,2,0:T(2,128)(2,1)S(1)}, u32[]{:S(2)}, u32[]{:S(2)}) async-start(bf16[16,2,168,168]{3,1,2,0:T(2,128)(2,1)} %copy.17), calls=%async_computation.2 | async-start | bytes 5505024 | tf_op jit(solution)/shard_map/all_to_all | solution.py:123
  399.1 97.5 %reduce-scatter.4.cloned.1.call-start = ((), (), s32[]{:S(2)}) async-start(), calls=%async_computation.4 | async-start | bytes 589824
  453.2 45.0 %copy-start.1 = (bf16[16,1681]{1,0:T(8,128)(2,1)S(1)}, bf16[16,1681]{1,0:T(8,128)(2,1)}, u32[]{:S(2)}) copy-start(bf16[16,1681]{1,0:T(8,128)(2,1)} %param.15) | copy-start | bytes 161380
  453.5 3.0 collective-permute-start
  454.8 6.0 %collective-permute-start.1 = (bf16[20,1024]{1,0:T(8,128)(2,1)S(1)}, bf16[20,1024]{1,0:T(8,128)(2,1)S(1)}, u32[]{:S(2)}, u32[]{:S(2)}) collective-permute-start(bf16[20,1024]{1,0:T(8,128)(2,1)S(1)} %get-tuple-element.172), channel_id=1, source_target_pairs={{8,0},{16,8},{24,16},{32,24},{40,32},{48,40},{56,48},{64,56},{72,6... | collective-permute-start | bytes 122888 | tf_op jit(solution)/shard_map/ppermute | solution.py:16
Sparse Core Ops, SparseCore 0:
  462.2 34.3 reduce-scatter.3
